TPU v7x, 32 devices: a whole 2x2x4 slice. The times are simulated.
32 devices in a mesh: group: 2 (over y), tm: 4 (over x, core), row: 4 (over z).
Axes of the slice: x: 2, y: 2, z: 4, core: 2. Of those that a mesh axis runs over, the one named last changes fastest.
Arguments:
- traces: bfloat16 [4096, 1024], P('row', ('group', 'tm')), parts along dimension 1, may hold values from -6 to 6
- weights: bfloat16 [4, 4096, 4096], P(None, 'row'), may hold values from -0.09375 to 0.09375
- pattern: int32 [4, 32, 32], replicated, may hold values 0 or 1
- cluster: int32 [4096], replicated, may hold values from 0 to 31
- element_damping_rate: float32 [4096], replicated, may hold values from 0 to 0.034, as said below
- local_step_length: float32 [512], P('tm'), may hold values from 0.4 to 1.9, as said below
- housing_keep_share: float32 [512], P('tm'), may hold values from 0.2 to 1, as said below
- admittance: float32 [4096], replicated, may hold values from 0.5 to 2
Outputs:
- adjoint_state: float32 [4096, 1024], P('row', ('group', 'tm')), parts along dimension 1
- pressure: bfloat16 [4096, 1024], P('row', ('group', 'tm')), parts along dimension 1
There are 2 independent parts, one for each index of `group`. A program takes and returns all parts, laid end to end along the dimension named above; an argument that names none is the same for every part. Nothing has to cross between parts.
Inputs may be any that keep to these rules, and one draw needn't show every extreme that they name: `element_damping_rate`: damping rates, positive. `local_step_length`: positive step lengths. `housing_keep_share`: kept shares, positive.
All inputs are finite; a program needn't handle non-finite values.
Results may differ from a plain program's by a relative error of at most 0.012.
Values may be sent and summed in bfloat16 or wider, within the bound.
No kernel may reach another device: no remote copies, remote signals or barrier semaphores. Data moves between devices by JAX's collectives and lax.ppermute only.
A program may use at most 192 MiB of HBM per device.

v0:
```python
import jax
import jax.numpy as jnp
from jax import lax
from jax.sharding import PartitionSpec as P


def carried_in(array, axis, join, neutral):
    count = lax.axis_size(axis)
    place = lax.axis_index(axis)
    ahead = count - 1 - place
    gathered = jax.tree.map(
        lambda a, kind: lax.all_gather(a.astype(kind), axis),
        array,
        jax.tree.map(lambda a: jnp.bfloat16 if a.dtype == jnp.float32 else a.dtype, array),
    )
    state = jax.tree.map(lambda a, e: jnp.zeros_like(a) + jnp.asarray(e, a.dtype), array, neutral)

    def one(hop, state):
        source = count - 1 - hop
        return join(
            state,
            jax.tree.map(
                lambda a, own: lax.dynamic_index_in_dim(a, source, 0, False).astype(own.dtype),
                gathered,
                array,
            ),
        )

    return lax.fori_loop(0, ahead, one, state)


def from_behind(array, axis, by):
    count = lax.axis_size(axis)
    pairs = [(i, i + by) for i in range(count) if 0 <= i + by < count]
    return lax.ppermute(array, axis, pairs)


def lag_kernels(weights, pattern, cluster, first_row):
    local_rows = weights.shape[1]
    own_labels = lax.dynamic_slice_in_dim(cluster, first_row, local_rows, 0)
    labels = jnp.arange(pattern.shape[1], dtype=jnp.int32)
    row_onehot = (own_labels[:, None] == labels[None, :]).astype(jnp.bfloat16)
    column_onehot = (labels[:, None] == cluster[None, :]).astype(jnp.bfloat16)
    kernels = []
    for lag_index in range(weights.shape[0]):
        picked = jnp.dot(
            row_onehot, pattern[lag_index].astype(jnp.bfloat16), preferred_element_type=jnp.float32
        )
        table = jnp.dot(
            picked.astype(jnp.bfloat16), column_onehot, preferred_element_type=jnp.float32
        )
        kernels.append(weights[lag_index] * table.astype(jnp.bfloat16))
    return kernels


def correlate(kernels, extended):
    length = extended.shape[1] - len(kernels) + 1
    running = None
    for lag_index in range(len(kernels)):
        columns = kernels[lag_index]
        product_term = lax.dot_general(
            columns,
            extended[:, lag_index : lag_index + length],
            (((0,), (0,)), ((), ())),
            preferred_element_type=jnp.float32,
        )
        running = product_term if running is None else running + product_term
    return running


def reconstruct(kernels, extended, running):
    number_of_lags = len(kernels)
    length = extended.shape[1] - number_of_lags + 1
    col_count = extended.shape[0]
    for lag_index in range(number_of_lags):
        columns = lax.slice_in_dim(kernels[lag_index], 0, col_count, axis=1)
        offset = number_of_lags - 1 - lag_index
        running = running + jnp.dot(
            columns, extended[:, offset : offset + length], preferred_element_type=jnp.float32
        )
    return running


def chain_step(earlier, later):
    return (later[0] * earlier[0], later[1] + later[0] * earlier[1])


def block_recurrence(keep_fraction, inflow):
    elements = keep_fraction.shape[0]
    length = keep_fraction.shape[1]
    span = 8
    keep_rows = keep_fraction.T.reshape(length // span, span, elements)
    inflow_rows = inflow.T.reshape(length // span, span, elements)

    def advance(carry, pieces):
        kept_now, state_now = carry
        keep_block, inflow_block = pieces
        kept_list = [None] * span
        state_list = [None] * span
        for inner in range(span - 1, -1, -1):
            state_now = keep_block[inner] * state_now + inflow_block[inner]
            kept_now = keep_block[inner] * kept_now
            kept_list[inner] = kept_now
            state_list[inner] = state_now
        return ((kept_now, state_now), (jnp.stack(kept_list, 0), jnp.stack(state_list, 0)))

    start = (jnp.ones((elements,), jnp.float32), jnp.zeros((elements,), jnp.float32))
    _, outputs = lax.scan(advance, start, (keep_rows, inflow_rows), reverse=True)
    retained = outputs[0].reshape(length, elements).T
    partial_state = outputs[1].reshape(length, elements).T
    return (retained, partial_state)


def forward_step(
    adjoint_total_sum,
    element_damping_rate,
    local_step_length,
    housing_keep_share,
    admittance,
    number_of_lags,
):
    length = adjoint_total_sum.shape[1]
    distribute_rows = element_damping_rate[:, None] * local_step_length[None, :]
    keep_fraction = jnp.exp(-distribute_rows) * housing_keep_share[None, :]
    inflow = jnp.sqrt(-jnp.expm1(-2.0 * distribute_rows)) * adjoint_total_sum
    retained, partial_state = block_recurrence(keep_fraction, inflow)
    neutral = (jnp.ones_like(retained[:, 0]), jnp.zeros_like(partial_state[:, 0]))
    incoming = carried_in((retained[:, 0], partial_state[:, 0]), "tm", chain_step, neutral)
    adj_state = partial_state + retained * incoming[1][:, None]
    driving = (admittance[:, None] * adj_state).astype(jnp.bfloat16)
    leading = from_behind(driving[:, length - number_of_lags + 1 :], "tm", 1)
    return (adj_state, jnp.concatenate([leading, driving], 1))


def local(
    traces,
    weights,
    pattern,
    cluster,
    element_damping_rate,
    local_step_length,
    housing_keep_share,
    admittance,
):
    local_rows = traces.shape[0]
    length = traces.shape[1]
    number_of_lags = weights.shape[0]
    first_row = lax.axis_index("row") * local_rows
    kernels = lag_kernels(weights, pattern, cluster, first_row)
    trailing = from_behind(traces[:, : number_of_lags - 1], "tm", -1)
    extended = jnp.concatenate([traces, trailing], 1)
    empty = jnp.zeros((local_rows, length), jnp.float32)
    adjoint_total_sum = lax.psum(correlate(kernels, extended).astype(jnp.bfloat16), "row").astype(
        jnp.float32
    )
    adj_state, driving = forward_step(
        adjoint_total_sum,
        element_damping_rate,
        local_step_length,
        housing_keep_share,
        admittance,
        number_of_lags,
    )
    pressure = reconstruct(kernels, driving, empty)
    adj_state = lax.dynamic_slice_in_dim(adj_state, first_row, local_rows, 0)
    return (adj_state, pressure.astype(jnp.bfloat16))


def solution(mesh):
    placed = (P("row", ("group", "tm")), P(None, "row", None), P(), P(), P(), P("tm"), P("tm"), P())
    return jax.shard_map(
        local,
        mesh=mesh,
        in_specs=placed,
        out_specs=(P("row", ("group", "tm")), P("row", ("group", "tm"))),
        check_vma=False,
    )
```

profile of v0, /device:TPU:1, one launch (start us, length us, event | category | flops | bytes accessed | tf_op | source)
XLA Modules:
  0.0 235.5 jit_solution(9270569396340060062)
XLA Ops:
  7.2 2.0 collective-permute-start
  9.2 0.8 convert.14
  10.0 0.7 dynamic_slice.40
  10.7 8.1 %bitcast_multiply_fusion.3 = bf16[1024,4096]{1,0:T(8,128)(2,1)} fusion(bf16[4,1024,4096]{2,1,0:T(8,128)(2,1)} %param.13, s32[4096]{0:T(1024)} %param.15, s32[1024]{0:T(1024)S(1)} %dynamic_slice.40, bf16[4,32,32]{2,1,0:T(8,128)(2,1)S(1)} %convert.14), kind=kOutput, calls=%fused_computation.34 | convolution fusion | flops 291700736 | bytes 16805888 | tf_op jit(solution)/shard_map/dot_general | solution.py:49
  18.8 7.2 %bitcast_multiply_fusion.2 = bf16[1024,4096]{1,0:T(8,128)(2,1)} fusion(bf16[4,1024,4096]{2,1,0:T(8,128)(2,1)} %param.13, s32[4096]{0:T(1024)S(1)} %copy-done.2, s32[1024]{0:T(1024)S(1)} %dynamic_slice.40, bf16[4,32,32]{2,1,0:T(8,128)(2,1)S(1)} %convert.14), kind=kOutput, calls=%fused_computation.33 | convolution fusion | flops 291700736 | bytes 16805888 | tf_op jit(solution)/shard_map/dot_general | solution.py:49
  26.0 7.1 %bitcast_multiply_fusion = bf16[1024,4096]{1,0:T(8,128)(2,1)} fusion(bf16[4,1024,4096]{2,1,0:T(8,128)(2,1)} %param.13, s32[4096]{0:T(1024)S(1)} %copy-done.2, s32[1024]{0:T(1024)S(1)} %dynamic_slice.40, bf16[4,32,32]{2,1,0:T(8,128)(2,1)S(1)} %convert.14), kind=kOutput, calls=%fused_computation.31 | convolution fusion | flops 291700736 | bytes 16805888 | tf_op jit(solution)/shard_map/dot_general | solution.py:49
  33.1 7.2 %bitcast_multiply_fusion.1 = bf16[1024,4096]{1,0:T(8,128)(2,1)} fusion(bf16[4,1024,4096]{2,1,0:T(8,128)(2,1)} %param.13, s32[4096]{0:T(1024)S(1)} %copy-done.2, s32[1024]{0:T(1024)S(1)} %dynamic_slice.40, bf16[4,32,32]{2,1,0:T(8,128)(2,1)S(1)} %convert.14), kind=kOutput, calls=%fused_computation.32 | convolution fusion | flops 291700736 | bytes 16805888 | tf_op jit(solution)/shard_map/dot_general | solution.py:49
  40.3 6.0 %fusion.42 = f32[4096,128]{1,0:T(8,128)S(1)} fusion(bf16[1024,4096]{1,0:T(8,128)(2,1)} %bitcast_multiply_fusion.3, bf16[1024,128]{1,0:T(8,128)(2,1)S(1)} %copy-done.1), kind=kOutput, calls=%fused_computation.94 | convolution fusion | flops 1073741824 | bytes 10747904 | tf_op jit(solution)/shard_map/dot_general | solution.py:61
  46.4 2.6 %fusion.20 = f32[4096,128]{1,0:T(8,128)S(1)} fusion(bf16[1024,4096]{1,0:T(8,128)(2,1)S(1)} %copy-done, bf16[1024,131]{1,0:T(8,128)(2,1)S(1)} %constant_dynamic-update-slice_fusion), kind=kOutput, calls=%fused_computation.72 | convolution fusion | flops 1073741824 | bytes 10747904 | tf_op jit(solution)/shard_map/dot_general | solution.py:61
  49.0 2.5 %convolution_add_fusion.1 = f32[4096,128]{1,0:T(8,128)S(1)} fusion(f32[4096,128]{1,0:T(8,128)S(1)} %fusion.42, bf16[1024,4096]{1,0:T(8,128)(2,1)S(1)} %bitcast.168, bf16[1024,131]{1,0:T(8,128)(2,1)S(1)} %constant_dynamic-update-slice_fusion), kind=kOutput, calls=%fused_computation.37 | convolution fusion | flops 1074266112 | bytes 12845056 | tf_op jit(solution)/shard_map/dot_general | solution.py:61
  51.7 3.6 %fusion.2 = bf16[4096,128]{1,0:T(8,128)(2,1)} fusion(f32[4096,128]{1,0:T(8,128)S(1)} %fusion.20, f32[4096,128]{1,0:T(8,128)S(1)} %convolution_add_fusion.1, bf16[1024,4096]{1,0:T(8,128)(2,1)S(1)} %bitcast.170, bf16[1024,131]{1,0:T(8,128)(2,1)S(1)} %constant_dynamic-update-slice_fusion), kind=kOutput, calls=%fused_computation.38 | convolution fusion | flops 1075314688 | bytes 13893632 | tf_op jit(solution)/shard_map/dot_general | solution.py:61
  55.4 1.6 exponential_multiply_fusion
  57.1 52.5 %all-reduce.2.cloned.1.call-done = bf16[4096,128]{1,0:T(8,128)(2,1)} async-done(((bf16[4096,128]{1,0:T(8,128)(2,1)}), bf16[4096,128]{1,0:T(8,128)(2,1)}) %all-reduce.2.cloned.1.call-update) | async-done | bytes 1048592 | tf_op jit(solution)/shard_map/psum | solution.py:153
  109.6 2.6 %multiply_bitcast_fusion = f32[128,4096]{0,1:T(8,128)S(1)} fusion(bf16[4096,128]{1,0:T(8,128)(2,1)} %all-reduce.2.cloned.1.call-done, f32[128]{0:T(128)S(1)} %copy-done.5, f32[4096]{0:T(1024)S(1)} %copy-done.3), kind=kLoop, calls=%fused_computation.44 | loop fusion | flops 2621440 | bytes 3162624 | tf_op jit(solution)/shard_map/transpose | solution.py:93
  112.2 1.9 copy.13
  114.3 1.5 broadcast.27.clone
  115.8 72.6 %while.36 = (s32[]{:T(128)}, f32[4096]{0:T(1024)S(1)}, f32[4096]{0:T(1024)S(1)}, f32[16,8,4096]{2,1,0:T(8,128)S(1)}, f32[16,8,4096]{2,1,0:T(8,128)}, /*index=5*/...) while((s32[]{:T(128)}, f32[4096]{0:T(1024)S(1)}, ...), condition=%wide.region_2.3_spmd.clone, body=%wide.region_1.2_spmd.clone.sunk | while | flops 106507 | bytes 2130251 | solution.py:108
  115.8 1.6 constant_dynamic-slice_fusion.18
  117.4 1.9 constant_dynamic-slice_fusion.19
  119.8 0.7 bitcast_dynamic-update-slice_fusion.3
  120.5 1.6 constant_dynamic-slice_fusion.18
  122.1 1.6 constant_dynamic-slice_fusion.19
  124.9 1.6 constant_dynamic-slice_fusion.18
  126.5 1.6 constant_dynamic-slice_fusion.19
  129.3 1.8 constant_dynamic-slice_fusion.18
  131.1 1.9 constant_dynamic-slice_fusion.19
  133.6 0.7 bitcast_dynamic-update-slice_fusion.3
  134.2 1.6 constant_dynamic-slice_fusion.18
  135.8 1.6 constant_dynamic-slice_fusion.19
  138.6 1.6 constant_dynamic-slice_fusion.18
  140.2 1.7 constant_dynamic-slice_fusion.19
  143.0 1.6 constant_dynamic-slice_fusion.18
  144.6 1.6 constant_dynamic-slice_fusion.19
  147.4 1.6 constant_dynamic-slice_fusion.18
  149.0 1.6 constant_dynamic-slice_fusion.19
  151.2 0.7 bitcast_dynamic-update-slice_fusion.3
  151.8 1.9 constant_dynamic-slice_fusion.18
  153.7 1.6 constant_dynamic-slice_fusion.19
  156.5 1.6 constant_dynamic-slice_fusion.18
  158.1 1.9 constant_dynamic-slice_fusion.19
  161.1 1.6 constant_dynamic-slice_fusion.18
  162.7 1.6 constant_dynamic-slice_fusion.19
  165.5 1.8 constant_dynamic-slice_fusion.18
  167.3 1.6 constant_dynamic-slice_fusion.19
  169.4 0.7 bitcast_dynamic-update-slice_fusion.3
  170.1 1.6 constant_dynamic-slice_fusion.18
  171.7 1.9 constant_dynamic-slice_fusion.19
  174.1 0.7 bitcast_dynamic-update-slice_fusion.3
  174.8 1.6 constant_dynamic-slice_fusion.18
  176.4 1.6 constant_dynamic-slice_fusion.19
  179.2 1.8 constant_dynamic-slice_fusion.18
  181.0 1.6 constant_dynamic-slice_fusion.19
  183.8 1.6 constant_dynamic-slice_fusion.18
  185.4 1.9 constant_dynamic-slice_fusion.19
  188.5 1.7 fusion.10
  190.2 5.5 %all-gather = bf16[16384,1]{0,1:T(2,128)(2,1)S(1)} all-gather(bf16[4096,1]{0,1:T(2,128)(2,1)S(1)} %slice.269), channel_id=2, replica_groups=mesh['group'=2,'tm'=4,'row'=4] {'tm'}, dimensions={0}, use_global_device_ids=true | all-gather | bytes 40960 | tf_op jit(solution)/shard_map/all_gather | solution.py:12
  196.1 5.2 %all-gather.1 = bf16[16384,1]{0,1:T(2,128)(2,1)S(1)} all-gather(bf16[4096,1]{0,1:T(2,128)(2,1)S(1)} %slice.270), channel_id=3, replica_groups=mesh['group'=2,'tm'=4,'row'=4] {'tm'}, dimensions={0}, use_global_device_ids=true | all-gather | bytes 40960 | tf_op jit(solution)/shard_map/all_gather | solution.py:12
  201.7 1.9 fusion.19
  203.7 5.7 %fusion.18 = f32[1024,128]{1,0:T(8,128)S(1)} fusion(bf16[1024,4096]{1,0:T(8,128)(2,1)} %bitcast_multiply_fusion.3, f32[128,4096]{1,0:T(8,128)S(1)} %get-tuple-element.305, f32[4096]{0:T(1024)S(1)} %copy-done.4), kind=kOutput, calls=%fused_computation.70 | convolution fusion | flops 1074790400 | bytes 11026432 | tf_op jit(solution)/shard_map/dot_general | solution.py:78
  209.5 3.1 %collective-permute-start.1 = (bf16[4096,3]{0,1:T(4,128)(2,1)S(1)}, bf16[4096,3]{0,1:T(4,128)(2,1)S(1)}, u32[]{:S(2)}, u32[]{:S(2)}) collective-permute-start(bf16[4096,3]{0,1:T(4,128)(2,1)S(1)} %slice.271), channel_id=1, source_target_pairs={{0,4},{4,8},{8,12},{1,5},{5,9},{9,13},{2,6},{6,10},{10,14},{3,7},{... | collective-permute-start | bytes 73736 | tf_op jit(solution)/shard_map/ppermute | solution.py:35
  212.6 1.0 copy.14
  213.6 5.9 %fusion.12 = f32[1024,128]{1,0:T(8,128)S(1)} fusion(bf16[1024,4096]{1,0:T(8,128)(2,1)} %bitcast_multiply_fusion, bf16[4096,128]{0,1:T(8,128)(2,1)S(1)} %get-tuple-element.304, bf16[4096,3]{0,1:T(4,128)(2,1)S(1)} %collective-permute-done.1), kind=kOutput, calls=%fused_computation.61 | convolution fusion | flops 1075838976 | bytes 9986048 | tf_op jit(solution)/shard_map/dot_general | solution.py:78
  219.5 6.0 %convolution_add_fusion.3 = f32[1024,128]{1,0:T(8,128)S(1)} fusion(f32[1024,128]{1,0:T(8,128)S(1)} %fusion.18, bf16[1024,4096]{1,0:T(8,128)(2,1)} %bitcast_multiply_fusion.2, bf16[4096,3]{0,1:T(4,128)(2,1)S(1)} %collective-permute-done.1, bf16[4096,128]{0,1:T(8,128)(2,1)S(1)} %get-tuple-element.304), kind=kOutput, calls=%fused_computation.50 | convolution fusion | flops 1075970048 | bytes 10510336 | tf_op jit(solution)/shard_map/dot_general | solution.py:78
  225.5 3.1 %fusion.5 = bf16[1024,128]{1,0:T(8,128)(2,1)} fusion(f32[1024,128]{1,0:T(8,128)S(1)} %fusion.12, f32[1024,128]{1,0:T(8,128)S(1)} %convolution_add_fusion.3, bf16[1024,4096]{1,0:T(8,128)(2,1)S(1)} %bitcast.172, bf16[4096,3]{0,1:T(4,128)(2,1)S(1)} %collective-permute-done.1, bf16[4096,128]{0,1:T(8,128)(2,1)S(1)} %get-tuple-element.304), kind=kOutput, calls=%fused_computation.51 | convolution fusion | flops 1076232192 | bytes 10772480 | tf_op jit(solution)/shard_map/dot_general | solution.py:78
  (114 shorter events, 16.1 us)
Async XLA Ops:
  7.2 102.4 %all-reduce.2.cloned.1.call-start = ((), (), s32[]{:S(2)}) async-start(), calls=%async_computation | async-start | bytes 2097152 | tf_op jit(solution)/shard_map/psum | solution.py:153
  7.2 39.1 %collective-permute-start = (bf16[1024,3]{1,0:T(8,128)(2,1)}, bf16[1024,3]{1,0:T(8,128)(2,1)S(1)}, u32[]{:S(2)}, u32[]{:S(2)}) collective-permute-start(bf16[1024,3]{1,0:T(8,128)(2,1)} %bitcast.208), channel_id=1, source_target_pairs={{4,0},{8,4},{12,8},{5,1},{9,5},{13,9},{6,2},{10,6},{14,10},{7,3},{... | collective-permute-start | bytes 18440 | tf_op jit(solution)/shard_map/ppermute | solution.py:35
  10.7 8.1 %copy-start.2 = (s32[4096]{0:T(1024)S(1)}, s32[4096]{0:T(1024)}, u32[]{:S(2)}) copy-start(s32[4096]{0:T(1024)} %param.15) | copy-start | bytes 49156
  33.1 7.2 %copy-start.1 = (bf16[1024,128]{1,0:T(8,128)(2,1)S(1)}, bf16[1024,128]{1,0:T(8,128)(2,1)}, u32[]{:S(2)}) copy-start(bf16[1024,128]{1,0:T(8,128)(2,1)} %param.12) | copy-start | bytes 786436
  40.3 6.1 %copy-start = (bf16[1024,4096]{1,0:T(8,128)(2,1)S(1)}, bf16[1024,4096]{1,0:T(8,128)(2,1)}, u32[]{:S(2)}) copy-start(bf16[1024,4096]{1,0:T(8,128)(2,1)} %bitcast_multiply_fusion) | copy-start | bytes 25165828
  40.3 8.7 %slice-start = ((s8[8388608]{0:T(1024)(128)(4,1)}), s8[4194304]{0:T(1024)(128)(4,1)S(1)}, s32[]{:S(2)}) async-start(s8[8388608]{0:T(1024)(128)(4,1)} %bitcast.167), calls=%async_computation.1 | async-start | bytes 8388608
  46.3 2.7 %slice-start.1 = ((s8[8388608]{0:T(1024)(128)(4,1)}), s8[4194304]{0:T(1024)(128)(4,1)S(1)}, s32[]{:S(2)}) async-start(s8[8388608]{0:T(1024)(128)(4,1)} %bitcast.167), calls=%async_computation.2 | async-start | bytes 8388608
  46.4 5.2 %slice-start.2 = ((s8[8388608]{0:T(1024)(128)(4,1)}), s8[4194304]{0:T(1024)(128)(4,1)S(1)}, s32[]{:S(2)}) async-start(s8[8388608]{0:T(1024)(128)(4,1)} %bitcast.169), calls=%async_computation.3 | async-start | bytes 8388608
  49.0 2.6 %slice-start.3 = ((s8[8388608]{0:T(1024)(128)(4,1)}), s8[4194304]{0:T(1024)(128)(4,1)S(1)}, s32[]{:S(2)}) async-start(s8[8388608]{0:T(1024)(128)(4,1)} %bitcast.169), calls=%async_computation.4 | async-start | bytes 8388608
  51.6 3.6 %copy-start.5 = (f32[128]{0:T(128)S(1)}, f32[128]{0:T(128)}, u32[]{:S(2)}) copy-start(f32[128]{0:T(128)} %param.17) | copy-start | bytes 1540
  51.6 3.7 %copy-start.6 = (f32[128]{0:T(128)S(1)}, f32[128]{0:T(128)}, u32[]{:S(2)}) copy-start(f32[128]{0:T(128)} %param.18) | copy-start | bytes 1540
  51.6 3.8 %copy-start.3 = (f32[4096]{0:T(1024)S(1)}, f32[4096]{0:T(1024)}, u32[]{:S(2)}) copy-start(f32[4096]{0:T(1024)} %param.16) | copy-start | bytes 49156
  195.9 5.8 %copy-start.4 = (f32[4096]{0:T(1024)S(1)}, f32[4096]{0:T(1024)}, u32[]{:S(2)}) copy-start(f32[4096]{0:T(1024)} %param.19) | copy-start | bytes 49156
  209.5 4.1 %collective-permute-start.1 = (bf16[4096,3]{0,1:T(4,128)(2,1)S(1)}, bf16[4096,3]{0,1:T(4,128)(2,1)S(1)}, u32[]{:S(2)}, u32[]{:S(2)}) collective-permute-start(bf16[4096,3]{0,1:T(4,128)(2,1)S(1)} %slice.271), channel_id=1, source_target_pairs={{0,4},{4,8},{8,12},{1,5},{5,9},{9,13},{2,6},{6,10},{10,14},{3,7},{... | collective-permute-start | bytes 73736 | tf_op jit(solution)/shard_map/ppermute | solution.py:35
  213.6 11.9 %slice-start.4 = ((s8[8388608]{0:T(1024)(128)(4,1)}), s8[4194304]{0:T(1024)(128)(4,1)S(1)}, s32[]{:S(2)}) async-start(s8[8388608]{0:T(1024)(128)(4,1)} %bitcast.171), calls=%async_computation.5 | async-start | bytes 8388608
  219.5 6.0 %slice-start.5 = ((s8[8388608]{0:T(1024)(128)(4,1)}), s8[4194304]{0:T(1024)(128)(4,1)S(1)}, s32[]{:S(2)}) async-start(s8[8388608]{0:T(1024)(128)(4,1)} %bitcast.171), calls=%async_computation.6 | async-start | bytes 8388608
Sparse Core Ops, SparseCore 0:
  55.4 54.2 all-reduce.1
where the time goes:
time: 237 us; the launch traced here: 235 us
  local copies, waits for them, and re-layouts  77 us (32%)
  matrix products  64.9 us (27%)
  waiting for transfers between devices  52.5 us (22%)
  between operations  14.4 us (6%)
  blocking collectives  10.8 us (5%)
  other arithmetic  10.2 us (4%)
  starting transfers between devices  5.08 us (2%)
    psum x1, waiting for transfers between devices, local(): lax.psum(correlate(kernels, extended).astype(jnp.bfloat16), 'row')  52.5 us
    dot_general x4, matrix products, lag_kernels(): jnp.dot(picked.astype(jnp.bfloat16), column_onehot, preferred_element_typ...  29.6 us
    slice x16, local copies, waits for them, and re-layouts, advance(): kept_now = keep_block[inner] * kept_now  27.4 us
    slice x16, local copies, waits for them, and re-layouts, advance(): state_now = keep_block[inner] * state_now + inflow_block[inner]  26.7 us
    dot_general x4, matrix products, reconstruct(): jnp.dot(columns, extended[:, offset:offset + length], preferred_element_t...  20.7 us
    dot_general x4, matrix products, correlate(): lax.dot_general(columns, extended[:, lag_index:lag_index + length], (((0,...  14.6 us
    all_gather x2, blocking collectives, carried_in(): lax.all_gather(a.astype(kind), axis)  10.8 us
    dynamic_update_slice x16, local copies, waits for them, and re-layouts, block_recurrence(): lax.scan(advance, start, (keep_rows, inflow_rows), reverse=True)  10.7 us
  transfers between devices with their start and end apart: 3, of which 1 were waited for; matrix products, arithmetic and copies ran while one was open for 17% of the time, Pallas kernels for 0%

commit v1 on v0

--- a/solution.py
+++ b/solution.py
@@ -150,9 +150,9 @@
     trailing = from_behind(traces[:, : number_of_lags - 1], "tm", -1)
     extended = jnp.concatenate([traces, trailing], 1)
     empty = jnp.zeros((local_rows, length), jnp.float32)
-    adjoint_total_sum = lax.psum(correlate(kernels, extended).astype(jnp.bfloat16), "row").astype(
-        jnp.float32
-    )
+    adjoint_total_sum = jnp.sum(
+        lax.all_gather(correlate(kernels, extended).astype(jnp.bfloat16), "row"), axis=0
+    ).astype(jnp.float32)
     adj_state, driving = forward_step(
         adjoint_total_sum,
         element_damping_rate,

time: 237 us -> 270 us (1.14)
  waiting for transfers between devices: 52.5 us -> 81.3 us
  other arithmetic: 10.2 us -> 12.9 us
    all_gather x0 -> x1, waiting for transfers between devices: none -> 81.2 us  [local(): lax.all_gather(correlate(kernels, extended).astype(jnp.bfloat16), 'row')]
    psum x1 -> x0, waiting for transfers between devices: 52.5 us -> none  [local(): lax.psum(correlate(kernels, extended).astype(jnp.bfloat16), 'row')]
    reduce_sum x0 -> x1, other arithmetic: none -> 3.47 us  [local(): jnp.sum(lax.all_gather(correlate(kernels, extended).astype(jnp.bfloat16),...]
  transfers between devices with their start and end apart: 3 -> 3, of which waited for: 1 -> 1; matrix products, arithmetic and copies ran while one was open for 17% -> 15% of each run, Pallas kernels for 0% -> 0%
where the time goes in v1:
time: 270 us; the launch traced here: 269 us
  waiting for transfers between devices  81.3 us (30%)
  local copies, waits for them, and re-layouts  77.3 us (29%)
  matrix products  66.2 us (25%)
  between operations  14.4 us (5%)
  other arithmetic  12.9 us (5%)
  blocking collectives  11 us (4%)
  starting transfers between devices  5.38 us (2%)
    all_gather x1, waiting for transfers between devices, local(): lax.all_gather(correlate(kernels, extended).astype(jnp.bfloat16), 'row')  81.2 us
    dot_general x4, matrix products, lag_kernels(): jnp.dot(picked.astype(jnp.bfloat16), column_onehot, preferred_element_typ...  30.9 us
    slice x16, local copies, waits for them, and re-layouts, advance(): kept_now = keep_block[inner] * kept_now  27.3 us
    slice x16, local copies, waits for them, and re-layouts, advance(): state_now = keep_block[inner] * state_now + inflow_block[inner]  27.1 us
    dot_general x4, matrix products, reconstruct(): jnp.dot(columns, extended[:, offset:offset + length], preferred_element_t...  20.7 us
    dot_general x4, matrix products, correlate(): lax.dot_general(columns, extended[:, lag_index:lag_index + length], (((0,...  14.6 us
    all_gather x2, blocking collectives, carried_in(): lax.all_gather(a.astype(kind), axis)  11 us
    dynamic_update_slice x16, local copies, waits for them, and re-layouts, block_recurrence(): lax.scan(advance, start, (keep_rows, inflow_rows), reverse=True)  10.7 us
  transfers between devices with their start and end apart: 3, of which 1 were waited for; matrix products, arithmetic and copies ran while one was open for 15% of the time, Pallas kernels for 0%

profile of v1, /device:TPU:1, one launch (start us, length us, event | category | flops | bytes accessed | tf_op | source)
XLA Modules:
  0.0 269.0 jit_solution(10388991343638829372)
XLA Ops:
  7.2 2.0 collective-permute-start
  9.2 0.8 convert.16
  10.0 0.7 dynamic_slice.40
  10.7 8.4 %bitcast_multiply_fusion.3 = bf16[1024,4096]{1,0:T(8,128)(2,1)} fusion(bf16[4,1024,4096]{2,1,0:T(8,128)(2,1)} %param.13, s32[4096]{0:T(1024)} %param.15, s32[1024]{0:T(1024)S(1)} %dynamic_slice.40, bf16[4,32,32]{2,1,0:T(8,128)(2,1)S(1)} %convert.16), kind=kOutput, calls=%fused_computation.34 | convolution fusion | flops 291700736 | bytes 16805888 | tf_op jit(solution)/shard_map/dot_general | solution.py:49
  19.1 7.5 %bitcast_multiply_fusion.2 = bf16[1024,4096]{1,0:T(8,128)(2,1)} fusion(bf16[4,1024,4096]{2,1,0:T(8,128)(2,1)} %param.13, s32[4096]{0:T(1024)S(1)} %copy-done.2, s32[1024]{0:T(1024)S(1)} %dynamic_slice.40, bf16[4,32,32]{2,1,0:T(8,128)(2,1)S(1)} %convert.16), kind=kOutput, calls=%fused_computation.33 | convolution fusion | flops 291700736 | bytes 16805888 | tf_op jit(solution)/shard_map/dot_general | solution.py:49
  26.6 7.4 %bitcast_multiply_fusion = bf16[1024,4096]{1,0:T(8,128)(2,1)} fusion(bf16[4,1024,4096]{2,1,0:T(8,128)(2,1)} %param.13, s32[4096]{0:T(1024)S(1)} %copy-done.2, s32[1024]{0:T(1024)S(1)} %dynamic_slice.40, bf16[4,32,32]{2,1,0:T(8,128)(2,1)S(1)} %convert.16), kind=kOutput, calls=%fused_computation.31 | convolution fusion | flops 291700736 | bytes 16805888 | tf_op jit(solution)/shard_map/dot_general | solution.py:49
  34.1 7.5 %bitcast_multiply_fusion.1 = bf16[1024,4096]{1,0:T(8,128)(2,1)} fusion(bf16[4,1024,4096]{2,1,0:T(8,128)(2,1)} %param.13, s32[4096]{0:T(1024)S(1)} %copy-done.2, s32[1024]{0:T(1024)S(1)} %dynamic_slice.40, bf16[4,32,32]{2,1,0:T(8,128)(2,1)S(1)} %convert.16), kind=kOutput, calls=%fused_computation.32 | convolution fusion | flops 291700736 | bytes 16805888 | tf_op jit(solution)/shard_map/dot_general | solution.py:49
  41.6 6.0 %fusion.42 = f32[4096,128]{1,0:T(8,128)S(1)} fusion(bf16[1024,4096]{1,0:T(8,128)(2,1)} %bitcast_multiply_fusion.3, bf16[1024,128]{1,0:T(8,128)(2,1)S(1)} %copy-done.1), kind=kOutput, calls=%fused_computation.94 | convolution fusion | flops 1073741824 | bytes 10747904 | tf_op jit(solution)/shard_map/dot_general | solution.py:61
  47.7 2.6 fusion.20
  50.3 2.5 convolution_add_fusion.1
  53.0 3.5 %fusion.2 = bf16[4096,128]{1,0:T(8,128)(2,1)} fusion(f32[4096,128]{1,0:T(8,128)S(1)} %fusion.20, f32[4096,128]{1,0:T(8,128)S(1)} %convolution_add_fusion.1, bf16[1024,4096]{1,0:T(8,128)(2,1)S(1)} %bitcast.171, bf16[1024,131]{1,0:T(8,128)(2,1)S(1)} %constant_dynamic-update-slice_fusion), kind=kOutput, calls=%fused_computation.38 | convolution fusion | flops 1075314688 | bytes 13893632 | tf_op jit(solution)/shard_map/dot_general | solution.py:61
  56.7 1.7 exponential_multiply_fusion
  58.4 81.2 %all-gather.5.cloned.1.call-done = bf16[16384,128]{1,0:T(8,128)(2,1)} async-done(((bf16[4096,128]{1,0:T(8,128)(2,1)}), bf16[16384,128]{1,0:T(8,128)(2,1)}) %all-gather.5.cloned.1.call-update) | async-done | bytes 4194320 | tf_op jit(solution)/shard_map/all_gather | solution.py:154
  139.6 3.5 %reduce_sum.12 = bf16[4096,128]{1,0:T(8,128)(2,1)S(1)} reduce(bf16[4,4096,128]{2,1,0:T(8,128)(2,1)} %bitcast.174, bf16[]{:T(256)} %constant.91.clone.1), dimensions={0}, to_apply=%region_0.0 | reduce | flops 1572864 | bytes 5242882 | tf_op jit(solution)/shard_map/reduce_sum | solution.py:153
  143.1 1.8 bitcast_multiply_fusion.5
  144.9 1.8 copy.15
  146.9 1.6 broadcast.30.clone
  148.5 73.0 %while.36 = (s32[]{:T(128)}, f32[4096]{0:T(1024)S(1)}, f32[4096]{0:T(1024)S(1)}, f32[16,8,4096]{2,1,0:T(8,128)S(1)}, f32[16,8,4096]{2,1,0:T(8,128)}, /*index=5*/...) while((s32[]{:T(128)}, f32[4096]{0:T(1024)S(1)}, ...), condition=%wide.region_2.3_spmd.clone, body=%wide.region_1.2_spmd.clone.sunk | while | flops 106507 | bytes 2130251 | solution.py:108
  148.5 1.9 constant_dynamic-slice_fusion.18
  150.4 1.7 constant_dynamic-slice_fusion.19
  153.2 1.6 constant_dynamic-slice_fusion.18
  154.8 1.9 constant_dynamic-slice_fusion.19
  157.9 1.6 constant_dynamic-slice_fusion.18
  159.5 1.6 constant_dynamic-slice_fusion.19
  162.3 1.9 constant_dynamic-slice_fusion.18
  164.2 1.9 constant_dynamic-slice_fusion.19
  166.5 0.7 bitcast_dynamic-update-slice_fusion.3
  167.2 1.6 constant_dynamic-slice_fusion.18
  168.8 1.6 constant_dynamic-slice_fusion.19
  171.6 1.6 constant_dynamic-slice_fusion.18
  173.2 1.6 constant_dynamic-slice_fusion.19
  176.0 1.6 constant_dynamic-slice_fusion.18
  177.6 1.6 constant_dynamic-slice_fusion.19
  180.4 1.6 constant_dynamic-slice_fusion.18
  182.0 1.9 constant_dynamic-slice_fusion.19
  185.1 1.6 constant_dynamic-slice_fusion.18
  186.7 1.6 constant_dynamic-slice_fusion.19
  189.4 1.9 constant_dynamic-slice_fusion.18
  191.2 1.6 constant_dynamic-slice_fusion.19
  194.0 1.6 constant_dynamic-slice_fusion.18
  195.6 1.6 constant_dynamic-slice_fusion.19
  198.4 1.6 constant_dynamic-slice_fusion.18
  200.0 1.6 constant_dynamic-slice_fusion.19
  202.1 0.7 bitcast_dynamic-update-slice_fusion.3
  202.8 1.9 constant_dynamic-slice_fusion.18
  204.7 1.9 constant_dynamic-slice_fusion.19
  207.8 1.6 constant_dynamic-slice_fusion.18
  209.4 1.9 constant_dynamic-slice_fusion.19
  211.7 0.7 bitcast_dynamic-update-slice_fusion.3
  212.4 1.6 constant_dynamic-slice_fusion.18
  214.0 1.6 constant_dynamic-slice_fusion.19
  216.8 1.9 constant_dynamic-slice_fusion.18
  218.7 1.6 constant_dynamic-slice_fusion.19
  220.8 0.7 bitcast_dynamic-update-slice_fusion.3
  221.5 1.7 fusion.10
  223.2 5.7 %all-gather.1 = bf16[16384,1]{0,1:T(2,128)(2,1)S(1)} all-gather(bf16[4096,1]{0,1:T(2,128)(2,1)S(1)} %slice.269), channel_id=3, replica_groups=mesh['group'=2,'tm'=4,'row'=4] {'tm'}, dimensions={0}, use_global_device_ids=true | all-gather | bytes 40960 | tf_op jit(solution)/shard_map/all_gather | solution.py:12
  229.3 5.2 %all-gather.2 = bf16[16384,1]{0,1:T(2,128)(2,1)S(1)} all-gather(bf16[4096,1]{0,1:T(2,128)(2,1)S(1)} %slice.270), channel_id=4, replica_groups=mesh['group'=2,'tm'=4,'row'=4] {'tm'}, dimensions={0}, use_global_device_ids=true | all-gather | bytes 40960 | tf_op jit(solution)/shard_map/all_gather | solution.py:12
  234.9 1.9 fusion.19
  236.9 5.7 %fusion.18 = f32[1024,128]{1,0:T(8,128)S(1)} fusion(bf16[1024,4096]{1,0:T(8,128)(2,1)} %bitcast_multiply_fusion.3, f32[128,4096]{1,0:T(8,128)S(1)} %get-tuple-element.309, f32[4096]{0:T(1024)S(1)} %copy-done.4), kind=kOutput, calls=%fused_computation.70 | convolution fusion | flops 1074790400 | bytes 11026432 | tf_op jit(solution)/shard_map/dot_general | solution.py:78
  242.7 3.4 %collective-permute-start.1 = (bf16[4096,3]{0,1:T(4,128)(2,1)S(1)}, bf16[4096,3]{0,1:T(4,128)(2,1)S(1)}, u32[]{:S(2)}, u32[]{:S(2)}) collective-permute-start(bf16[4096,3]{0,1:T(4,128)(2,1)S(1)} %slice.271), channel_id=1, source_target_pairs={{0,4},{4,8},{8,12},{1,5},{5,9},{9,13},{2,6},{6,10},{10,14},{3,7},{... | collective-permute-start | bytes 73736 | tf_op jit(solution)/shard_map/ppermute | solution.py:35
  246.1 1.0 copy.16
  247.1 5.9 %fusion.12 = f32[1024,128]{1,0:T(8,128)S(1)} fusion(bf16[1024,4096]{1,0:T(8,128)(2,1)} %bitcast_multiply_fusion, bf16[4096,128]{0,1:T(8,128)(2,1)S(1)} %get-tuple-element.308, bf16[4096,3]{0,1:T(4,128)(2,1)S(1)} %collective-permute-done.1), kind=kOutput, calls=%fused_computation.61 | convolution fusion | flops 1075838976 | bytes 9986048 | tf_op jit(solution)/shard_map/dot_general | solution.py:78
  253.0 6.0 %convolution_add_fusion.3 = f32[1024,128]{1,0:T(8,128)S(1)} fusion(f32[1024,128]{1,0:T(8,128)S(1)} %fusion.18, bf16[1024,4096]{1,0:T(8,128)(2,1)} %bitcast_multiply_fusion.2, bf16[4096,3]{0,1:T(4,128)(2,1)S(1)} %collective-permute-done.1, bf16[4096,128]{0,1:T(8,128)(2,1)S(1)} %get-tuple-element.308), kind=kOutput, calls=%fused_computation.50 | convolution fusion | flops 1075970048 | bytes 10510336 | tf_op jit(solution)/shard_map/dot_general | solution.py:78
  259.0 3.1 %fusion.5 = bf16[1024,128]{1,0:T(8,128)(2,1)} fusion(f32[1024,128]{1,0:T(8,128)S(1)} %fusion.12, f32[1024,128]{1,0:T(8,128)S(1)} %convolution_add_fusion.3, bf16[1024,4096]{1,0:T(8,128)(2,1)S(1)} %bitcast.173, bf16[4096,3]{0,1:T(4,128)(2,1)S(1)} %collective-permute-done.1, bf16[4096,128]{0,1:T(8,128)(2,1)S(1)} %get-tuple-element.308), kind=kOutput, calls=%fused_computation.51 | convolution fusion | flops 1076232192 | bytes 10772480 | tf_op jit(solution)/shard_map/dot_general | solution.py:78
  (115 shorter events, 16.8 us)
Async XLA Ops:
  7.2 132.5 %all-gather.5.cloned.1.call-start = ((), (), s32[]{:S(2)}) async-start(), calls=%async_computation | async-start | bytes 5242880 | tf_op jit(solution)/shard_map/all_gather | solution.py:154
  7.2 40.4 %collective-permute-start = (bf16[1024,3]{1,0:T(8,128)(2,1)}, bf16[1024,3]{1,0:T(8,128)(2,1)S(1)}, u32[]{:S(2)}, u32[]{:S(2)}) collective-permute-start(bf16[1024,3]{1,0:T(8,128)(2,1)} %bitcast.210), channel_id=1, source_target_pairs={{4,0},{8,4},{12,8},{5,1},{9,5},{13,9},{6,2},{10,6},{14,10},{7,3},{... | collective-permute-start | bytes 18440 | tf_op jit(solution)/shard_map/ppermute | solution.py:35
  10.7 8.4 %copy-start.2 = (s32[4096]{0:T(1024)S(1)}, s32[4096]{0:T(1024)}, u32[]{:S(2)}) copy-start(s32[4096]{0:T(1024)} %param.15) | copy-start | bytes 49156
  34.1 7.5 %copy-start.1 = (bf16[1024,128]{1,0:T(8,128)(2,1)S(1)}, bf16[1024,128]{1,0:T(8,128)(2,1)}, u32[]{:S(2)}) copy-start(bf16[1024,128]{1,0:T(8,128)(2,1)} %param.12) | copy-start | bytes 786436
  41.6 6.1 %copy-start = (bf16[1024,4096]{1,0:T(8,128)(2,1)S(1)}, bf16[1024,4096]{1,0:T(8,128)(2,1)}, u32[]{:S(2)}) copy-start(bf16[1024,4096]{1,0:T(8,128)(2,1)} %bitcast_multiply_fusion) | copy-start | bytes 25165828
  41.6 8.7 %slice-start = ((s8[8388608]{0:T(1024)(128)(4,1)}), s8[4194304]{0:T(1024)(128)(4,1)S(1)}, s32[]{:S(2)}) async-start(s8[8388608]{0:T(1024)(128)(4,1)} %bitcast.168), calls=%async_computation.1 | async-start | bytes 8388608
  47.6 2.7 %slice-start.1 = ((s8[8388608]{0:T(1024)(128)(4,1)}), s8[4194304]{0:T(1024)(128)(4,1)S(1)}, s32[]{:S(2)}) async-start(s8[8388608]{0:T(1024)(128)(4,1)} %bitcast.168), calls=%async_computation.2 | async-start | bytes 8388608
  47.7 5.2 %slice-start.2 = ((s8[8388608]{0:T(1024)(128)(4,1)}), s8[4194304]{0:T(1024)(128)(4,1)S(1)}, s32[]{:S(2)}) async-start(s8[8388608]{0:T(1024)(128)(4,1)} %bitcast.170), calls=%async_computation.3 | async-start | bytes 8388608
  50.3 2.6 slice-start.3
  52.9 3.6 %copy-start.5 = (f32[128]{0:T(128)S(1)}, f32[128]{0:T(128)}, u32[]{:S(2)}) copy-start(f32[128]{0:T(128)} %param.17) | copy-start | bytes 1540
  52.9 3.7 %copy-start.6 = (f32[128]{0:T(128)S(1)}, f32[128]{0:T(128)}, u32[]{:S(2)}) copy-start(f32[128]{0:T(128)} %param.18) | copy-start | bytes 1540
  52.9 3.8 %copy-start.3 = (f32[4096]{0:T(1024)S(1)}, f32[4096]{0:T(1024)}, u32[]{:S(2)}) copy-start(f32[4096]{0:T(1024)} %param.16) | copy-start | bytes 49156
  229.1 5.8 %copy-start.4 = (f32[4096]{0:T(1024)S(1)}, f32[4096]{0:T(1024)}, u32[]{:S(2)}) copy-start(f32[4096]{0:T(1024)} %param.19) | copy-start | bytes 49156
  242.7 4.4 %collective-permute-start.1 = (bf16[4096,3]{0,1:T(4,128)(2,1)S(1)}, bf16[4096,3]{0,1:T(4,128)(2,1)S(1)}, u32[]{:S(2)}, u32[]{:S(2)}) collective-permute-start(bf16[4096,3]{0,1:T(4,128)(2,1)S(1)} %slice.271), channel_id=1, source_target_pairs={{0,4},{4,8},{8,12},{1,5},{5,9},{9,13},{2,6},{6,10},{10,14},{3,7},{... | collective-permute-start | bytes 73736 | tf_op jit(solution)/shard_map/ppermute | solution.py:35
  247.1 11.9 %slice-start.4 = ((s8[8388608]{0:T(1024)(128)(4,1)}), s8[4194304]{0:T(1024)(128)(4,1)S(1)}, s32[]{:S(2)}) async-start(s8[8388608]{0:T(1024)(128)(4,1)} %bitcast.172), calls=%async_computation.5 | async-start | bytes 8388608
  253.0 6.0 %slice-start.5 = ((s8[8388608]{0:T(1024)(128)(4,1)}), s8[4194304]{0:T(1024)(128)(4,1)S(1)}, s32[]{:S(2)}) async-start(s8[8388608]{0:T(1024)(128)(4,1)} %bitcast.172), calls=%async_computation.6 | async-start | bytes 8388608
Sparse Core Ops, SparseCore 0:
  56.6 82.9 all-gather.4
